TPU v7x, 512 devices: a whole 4x8x8 slice. The times are simulated.
512 devices in a mesh: seq: 32 (over x, y), chan: 16 (over z, core).
Axes of the slice: x: 4, y: 8, z: 8, core: 2. Of those that a mesh axis runs over, the one named last changes fastest.
Arguments:
- tokens: bfloat16 [1536, 16384], P('chan', 'seq'), may hold values from -6 to 6
- gate_weight: bfloat16 [1536, 1536], P('chan'), may hold values from -0.15625 to 0.15625
- value_weight: bfloat16 [1536, 1536], P('chan'), may hold values from -0.15625 to 0.15625
- first_factor: bfloat16 [64, 256, 256], P('seq'), may hold values from -0.375 to 0.375
- second_factor: bfloat16 [256, 64, 64], P('seq'), may hold values from -0.75 to 0.75
- down_latent: bfloat16 [1536, 128], P('chan'), may hold values from -0.15625 to 0.15625
- up_latent: bfloat16 [1536, 128], P('chan'), may hold values from -0.5 to 0.5
- doc_lengths: int32 [64], replicated, may hold values from 1 to 8704, 16384 in all
- cotangent: bfloat16 [1536, 16384], P('chan', 'seq'), may hold values from -6 to 6
Outputs:
- hidden: bfloat16 [1536, 16384], P('chan', 'seq')
- d_gate_weight: float32 [1536, 1536], P('chan')
- d_value_weight: float32 [1536, 1536], P('chan')
- d_first: float32 [64, 256, 256], P('seq', 'chan')
- d_second: float32 [256, 64, 64], P('seq', 'chan')
- d_down: float32 [1536, 128], P('chan')
- d_up: float32 [1536, 128], P('chan')
Inputs may be any that keep to these rules, and one draw needn't show every extreme that they name: `doc_lengths`: the documents' lengths sum to 16384; the longest is exactly 8704 tokens.
All inputs are finite; a program needn't handle non-finite values.
Results may differ from a plain program's by a relative error of at most 0.0058.
Values may be sent and summed in bfloat16 or wider, within the bound.
No kernel may reach another device: no remote copies, remote signals or barrier semaphores. Data moves between devices by JAX's collectives and lax.ppermute only.
A program may use at most 64 MiB of HBM per device.

v0:
```python
import jax
import jax.numpy as jnp
from jax import lax
from jax.sharding import PartitionSpec as P

HIGHEST = lax.Precision.HIGHEST


def seq_exchange(x):
    return lax.all_to_all(x, "seq", 0, 0, tiled=True)


def chan_exchange(x):
    return lax.all_to_all(x, "chan", 0, 0, tiled=True)


def split_hi_lo(x):
    hi = lax.reduce_precision(x, exponent_bits=8, mantissa_bits=7)
    lo = x - hi
    return jnp.concatenate([hi.astype(jnp.bfloat16), lo.astype(jnp.bfloat16)], axis=-1)


def join_hi_lo(x):
    n = x.shape[-1] // 2
    return x[..., :n].astype(jnp.float32) + x[..., n:].astype(jnp.float32)


def body(
    tokens,
    gate_weight,
    value_weight,
    first_factor,
    second_factor,
    down_latent,
    up_latent,
    doc_lengths,
    cotangent,
):
    n_seq = lax.axis_size("seq")
    n_chan = lax.axis_size("chan")
    chan_rows, tok_cols = tokens.shape
    blocks_here, block_width, _ = first_factor.shape
    k_here, n_blk2, _ = second_factor.shape
    lat = down_latent.shape[1]
    n_doc = doc_lengths.shape[0]
    docs_here = n_doc // n_seq
    me = lax.axis_index("seq")
    packed = jnp.concatenate([tokens, down_latent], axis=1)
    gathered_all = lax.all_gather(packed, "chan", axis=0, tiled=True)
    gathered = gathered_all[:, :tok_cols]
    down_full = gathered_all[:, tok_cols:]
    doc_ends = jnp.cumsum(doc_lengths)
    doc_begins = doc_ends - doc_lengths
    position = me * tok_cols + jnp.arange(tok_cols, dtype=jnp.int32)
    member = (
        (position[None, :] >= doc_begins[:, None]) & (position[None, :] < doc_ends[:, None])
    ).astype(jnp.float32)
    len_scale = lax.rsqrt(doc_lengths.astype(jnp.float32))
    gate_pre = jnp.dot(gate_weight, gathered, preferred_element_type=jnp.float32)
    value_bf = jnp.dot(value_weight, gathered, preferred_element_type=jnp.float32).astype(
        jnp.bfloat16
    )
    latent = jnp.einsum("ct,cl->lt", gathered, down_full, preferred_element_type=jnp.float32)
    doc_lat_part = jnp.einsum("dt,lt->dl", member, latent, precision=HIGHEST)
    xdoc_part = jnp.einsum(
        "ct,dt->cd", tokens, member.astype(jnp.bfloat16), preferred_element_type=jnp.float32
    )
    blocked = value_bf.reshape(chan_rows, blocks_here, block_width)
    inner_mix = jnp.einsum(
        "ikj,cij->ikc", first_factor, blocked, preferred_element_type=jnp.float32
    ).astype(jnp.bfloat16)
    sig = jax.nn.sigmoid(gate_pre)
    act = gate_pre * sig
    upstream = cotangent.astype(jnp.float32)
    d_mixed = upstream * act
    d_mixed_bf = d_mixed.astype(jnp.bfloat16)
    per_doc_part = jnp.einsum("ct,dt->cd", d_mixed, member, precision=HIGHEST)
    inner_send = inner_mix.reshape(blocks_here, n_seq, k_here, chan_rows).transpose(1, 0, 2, 3)
    d_send = d_mixed_bf.reshape(chan_rows, blocks_here, n_seq, k_here).transpose(2, 1, 3, 0)
    mix_send = jnp.concatenate([inner_send, d_send], axis=3).reshape(n_seq, -1)
    n_mix = mix_send.shape[1]
    small_send = jnp.concatenate(
        [
            doc_lat_part.reshape(n_seq, docs_here * lat),
            per_doc_part.reshape(chan_rows, n_seq, docs_here)
            .transpose(1, 0, 2)
            .reshape(n_seq, chan_rows * docs_here),
            xdoc_part.reshape(chan_rows, n_seq, docs_here)
            .transpose(1, 0, 2)
            .reshape(n_seq, chan_rows * docs_here),
        ],
        axis=1,
    )
    recv2 = seq_exchange(jnp.concatenate([mix_send, split_hi_lo(small_send)], axis=1))
    mix2 = recv2[:, :n_mix].reshape(n_seq, blocks_here, k_here, 2 * chan_rows)
    columns = mix2[..., :chan_rows].reshape(n_seq * blocks_here, k_here, chan_rows)
    d_outer = mix2[..., chan_rows:].reshape(n_seq * blocks_here, k_here, chan_rows)
    small_red = jnp.sum(join_hi_lo(recv2[:, n_mix:]), axis=0)
    n_a = docs_here * lat
    n_b = chan_rows * docs_here
    scale_here = lax.dynamic_slice(len_scale, (me * docs_here,), (docs_here,))
    pooled_here = small_red[:n_a].reshape(docs_here, lat) * scale_here[:, None]
    per_doc_here = small_red[n_a : n_a + n_b].reshape(chan_rows, docs_here)
    xdoc_here = small_red[n_a + n_b :].reshape(chan_rows, docs_here)
    up_float = up_latent.astype(jnp.float32)
    g_part = jnp.einsum("cd,cl->dl", per_doc_here, up_float, precision=HIGHEST)
    outer_mix = jnp.einsum(
        "kmi,ikc->mkc", second_factor, columns, preferred_element_type=jnp.float32
    ).astype(jnp.bfloat16)
    d_inner = jnp.einsum(
        "kmi,mkc->ikc", second_factor, d_outer, preferred_element_type=jnp.float32
    ).astype(jnp.bfloat16)
    d_second_part = jnp.einsum("mkc,ikc->kmi", d_outer, columns, preferred_element_type=jnp.float32)
    outer_send = outer_mix.reshape(n_seq, blocks_here, k_here, chan_rows)
    dinner_send = d_inner.reshape(n_seq, blocks_here, k_here, chan_rows)
    piece = jnp.concatenate(
        [
            pooled_here.reshape(n_a),
            per_doc_here.reshape(n_b),
            xdoc_here.reshape(n_b),
            g_part.reshape(n_a),
        ]
    )
    piece_b = jnp.broadcast_to(split_hi_lo(piece)[None, :], (n_seq, 2 * piece.shape[0]))
    send3 = jnp.concatenate(
        [jnp.concatenate([outer_send, dinner_send], axis=3).reshape(n_seq, -1), piece_b], axis=1
    )
    recv3_all = seq_exchange(send3)
    recv3 = recv3_all[:, :n_mix].reshape(n_seq, blocks_here, k_here, 2 * chan_rows)
    gath3 = join_hi_lo(recv3_all[:, n_mix:])
    outer_tok = (
        recv3[..., :chan_rows]
        .transpose(3, 1, 0, 2)
        .reshape(chan_rows, tok_cols)
        .astype(jnp.float32)
    )
    d_rows = (
        recv3[..., chan_rows:].transpose(1, 0, 2, 3).reshape(blocks_here, n_seq * k_here, chan_rows)
    )
    pooled = gath3[:, :n_a].reshape(n_doc, lat)
    per_doc = (
        gath3[:, n_a : n_a + n_b]
        .reshape(n_seq, chan_rows, docs_here)
        .transpose(1, 0, 2)
        .reshape(chan_rows, n_doc)
    )
    xdoc = (
        gath3[:, n_a + n_b : n_a + 2 * n_b]
        .reshape(n_seq, chan_rows, docs_here)
        .transpose(1, 0, 2)
        .reshape(chan_rows, n_doc)
    )
    g_gath = gath3[:, n_a + 2 * n_b :].reshape(1, n_doc * lat)
    spread = jnp.einsum("dl,cl->cd", pooled, up_float, precision=HIGHEST)
    summary = jnp.dot(spread, member, precision=HIGHEST)
    mixed = outer_tok + summary
    hidden = (act * mixed).astype(jnp.bfloat16)
    d_gate_bf = (upstream * mixed * sig * (1.0 + gate_pre * (1.0 - sig))).astype(jnp.bfloat16)
    d_value_bf = (
        jnp.einsum("ikj,ikc->cij", first_factor, d_rows, preferred_element_type=jnp.float32)
        .astype(jnp.bfloat16)
        .reshape(chan_rows, tok_cols)
    )
    d_first_part = jnp.einsum("ikc,cij->ikj", d_rows, blocked, preferred_element_type=jnp.float32)
    d_up = jnp.einsum("cd,dl->cl", per_doc, pooled, precision=HIGHEST)
    both_grads = jnp.concatenate([d_gate_bf, d_value_bf], axis=0)
    d_proj_part = jnp.einsum("ot,it->oi", both_grads, gathered, preferred_element_type=jnp.float32)
    rows_here = 2 * chan_rows // n_seq
    width = d_proj_part.shape[1]
    proj_send = d_proj_part.reshape(n_seq, rows_here, width).astype(jnp.bfloat16)
    proj_red = jnp.sum(seq_exchange(proj_send).astype(jnp.float32), axis=0)
    k_part = block_width // n_chan
    m_part = n_blk2 // n_chan
    first_send = (
        d_first_part.reshape(blocks_here, n_chan, k_part, block_width)
        .transpose(1, 0, 2, 3)
        .reshape(n_chan, -1)
    )
    second_send = (
        d_second_part.reshape(k_here, n_chan, m_part, n_blk2)
        .transpose(1, 0, 2, 3)
        .reshape(n_chan, -1)
    )
    g_send = jnp.broadcast_to(g_gath, (n_chan, n_doc * lat))
    fac_send = jnp.concatenate([first_send, second_send, g_send], axis=1)
    fac_red = lax.psum_scatter(
        fac_send.reshape(-1, 128), "chan", scatter_dimension=0, tiled=True
    ).reshape(-1)
    n_f = blocks_here * k_part * block_width
    d_first = fac_red[:n_f].reshape(blocks_here, k_part, block_width)
    n_s = k_here * m_part * n_blk2
    d_second = fac_red[n_f : n_f + n_s].reshape(k_here, m_part, n_blk2)
    g_full = fac_red[n_f + n_s :].reshape(n_doc, lat)
    gath5 = seq_exchange(jnp.broadcast_to(proj_red[None], (n_seq, rows_here, width)))
    d_proj = gath5.reshape(2 * chan_rows, width)
    d_pooled = g_full * len_scale[:, None]
    d_down = jnp.einsum(
        "cd,dl->cl", xdoc, d_pooled.astype(jnp.bfloat16).astype(jnp.float32), precision=HIGHEST
    )
    return (hidden, d_proj[:chan_rows], d_proj[chan_rows:], d_first, d_second, d_down, d_up)


def solution(mesh):
    in_specs = (
        P("chan", "seq"),
        P("chan", None),
        P("chan", None),
        P("seq", None, None),
        P("seq", None, None),
        P("chan", None),
        P("chan", None),
        P(),
        P("chan", "seq"),
    )
    out_specs = (
        P("chan", "seq"),
        P("chan", None),
        P("chan", None),
        P("seq", "chan", None),
        P("seq", "chan", None),
        P("chan", None),
        P("chan", None),
    )
    return jax.shard_map(body, mesh=mesh, in_specs=in_specs, out_specs=out_specs, check_vma=False)
```

profile of v0, /device:TPU:6, one launch (start us, length us, event | category | flops | bytes accessed | tf_op | source)
XLA Modules:
  0.0 200.5 jit_solution(10429211262752419553)
XLA Ops:
  7.2 1.6 pad_maximum_fusion.2
  10.5 1.1 fusion.27
  11.8 46.3 %all-gather.2.cloned.1.call-done = bf16[1536,640]{1,0:T(8,128)(2,1)} async-done(((bf16[96,640]{1,0:T(8,128)(2,1)}), bf16[1536,640]{1,0:T(8,128)(2,1)}) %all-gather.2.cloned.1.call-update) | async-done | bytes 1966096 | tf_op jit(solution)/shard_map/all_gather | solution.py:49
  58.1 1.9 convolution_convert_fusion.3
  60.4 2.0 fusion.3
  62.7 1.8 fusion.16
  67.8 9.9 %all-to-all-start = ((bf16[32,2,2176]{2,1,0:T(2,128)(2,1)}), bf16[32,2,2176]{2,1,0:T(2,128)(2,1)S(1)}, u32[]{:S(2)}, u32[]{:S(2)}) async-start(bf16[32,2,2176]{2,1,0:T(2,128)(2,1)} %reshape.228), calls=%async_computation | async-start | bytes 557056 | tf_op jit(solution)/shard_map/all_to_all | solution.py:10
  77.8 11.0 %all-to-all-done = bf16[32,2,2176]{2,1,0:T(2,128)(2,1)S(1)} async-done(((bf16[32,2,2176]{2,1,0:T(2,128)(2,1)}), bf16[32,2,2176]{2,1,0:T(2,128)(2,1)S(1)}, u32[]{:S(2)}, u32[]{:S(2)}) %all-to-all-start) | async-done | bytes 278560 | tf_op jit(solution)/shard_map/all_to_all | solution.py:10
  91.5 0.8 reduce.2
  93.1 6.5 %all-to-all-start.1 = ((bf16[32,2,2432]{2,1,0:T(2,128)(2,1)}), bf16[32,2,2432]{2,1,0:T(2,128)(2,1)S(1)}, u32[]{:S(2)}, u32[]{:S(2)}) async-start(bf16[32,2,2432]{2,1,0:T(2,128)(2,1)} %reshape.230), calls=%async_computation.1 | async-start | bytes 622592 | tf_op jit(solution)/shard_map/all_to_all | solution.py:10
  100.1 10.5 %all-to-all-done.1 = bf16[32,2,2432]{2,1,0:T(2,128)(2,1)S(1)} async-done(((bf16[32,2,2432]{2,1,0:T(2,128)(2,1)}), bf16[32,2,2432]{2,1,0:T(2,128)(2,1)S(1)}, u32[]{:S(2)}, u32[]{:S(2)}) %all-to-all-start.1) | async-done | bytes 311328 | tf_op jit(solution)/shard_map/all_to_all | solution.py:10
  112.3 1.0 fusion.10
  113.3 2.1 %convolution_convert_fusion = bf16[192,1536]{1,0:T(8,128)(2,1)S(1)} fusion(bf16[1536,640]{1,0:T(8,128)(2,1)} %all-gather.2.cloned.1.call-done, bf16[96,512]{1,0:T(8,128)(2,1)S(1)} %bitcast.139, bf16[96,512]{1,0:T(8,128)(2,1)S(1)} %get-tuple-element.9), kind=kOutput, calls=%fused_computation | convolution fusion | flops 302678016 | bytes 2359296 | tf_op jit(solution)/shard_map/ot,it->oi/dot_general | solution.py:167
  115.4 1.1 convert_element_type.128
  116.4 6.6 %all-to-all-start.2 = ((bf16[32,6,1536]{2,1,0:T(8,128)(2,1)}), bf16[32,6,1536]{2,1,0:T(8,128)(2,1)S(1)}, u32[]{:S(2)}, u32[]{:S(2)}) async-start(bf16[32,6,1536]{2,1,0:T(8,128)(2,1)} %convert_element_type.128), calls=%async_computation.2 | async-start | bytes 1572864 | tf_op jit(solution)/shard_map/all_to_all | solution.py:10
  123.5 1.2 reshape.217
  124.8 17.8 %all-to-all-done.2 = bf16[32,6,1536]{2,1,0:T(8,128)(2,1)S(1)} async-done(((bf16[32,6,1536]{2,1,0:T(8,128)(2,1)}), bf16[32,6,1536]{2,1,0:T(8,128)(2,1)S(1)}, u32[]{:S(2)}, u32[]{:S(2)}) %all-to-all-start.2) | async-done | bytes 589856 | tf_op jit(solution)/shard_map/all_to_all | solution.py:10
  142.8 1.3 broadcast_in_dim.9
  144.1 7.3 %all-to-all-start.3 = ((f32[32,6,1536]{2,1,0:T(8,128)}), f32[32,6,1536]{2,1,0:T(8,128)S(1)}, u32[]{:S(2)}, u32[]{:S(2)}) async-start(f32[32,6,1536]{2,1,0:T(8,128)} %broadcast_in_dim.9), calls=%async_computation.3 | async-start | bytes 3145728 | tf_op jit(solution)/shard_map/all_to_all | solution.py:10
  151.9 0.9 fusion.42
  152.8 34.6 %reduce-scatter.2.cloned.1.call-done = f32[144,128]{1,0:T(8,128)} async-done(((f32[2304,128]{1,0:T(8,128)}), f32[144,128]{1,0:T(8,128)}) %reduce-scatter.2.cloned.1.call-update) | async-done | bytes 73744 | tf_op jit(solution)/shard_map/reduce_scatter | solution.py:186
  190.1 1.6 fusion.29
  191.8 0.9 slice.126
  192.7 0.9 slice.124
  (98 shorter events, 15.1 us)
Async XLA Ops:
  7.2 55.5 %copy-start = (bf16[96,1536]{1,0:T(8,128)(2,1)S(1)}, bf16[96,1536]{1,0:T(8,128)(2,1)}, u32[]{:S(2)}) copy-start(bf16[96,1536]{1,0:T(8,128)(2,1)} %param.10) | copy-start | bytes 884740
  7.2 52.8 %copy-start.1 = (bf16[2,256,256]{2,1,0:T(8,128)(2,1)S(1)}, bf16[2,256,256]{2,1,0:T(8,128)(2,1)}, u32[]{:S(2)}) copy-start(bf16[2,256,256]{2,1,0:T(8,128)(2,1)} %param.12) | copy-start | bytes 786436
  7.2 50.9 %all-gather.2.cloned.1.call-start = ((), (), s32[]{:S(2)}) async-start(), calls=%async_computation.5 | async-start | bytes 2088960 | tf_op jit(solution)/shard_map/all_gather | solution.py:49
  60.0 2.6 %copy-start.5 = (bf16[96,512]{1,0:T(8,128)(2,1)S(1)}, bf16[96,512]{1,0:T(8,128)(2,1)}, u32[]{:S(2)}) copy-start(bf16[96,512]{1,0:T(8,128)(2,1)} %param.17) | copy-start | bytes 294916
  65.4 12.3 %copy-start.4 = (s32[64]{0:T(128)S(1)}, s32[64]{0:T(128)}, u32[]{:S(2)}) copy-start(s32[64]{0:T(128)} %param.16) | copy-start | bytes 772
  67.8 21.0 %all-to-all-start = ((bf16[32,2,2176]{2,1,0:T(2,128)(2,1)}), bf16[32,2,2176]{2,1,0:T(2,128)(2,1)S(1)}, u32[]{:S(2)}, u32[]{:S(2)}) async-start(bf16[32,2,2176]{2,1,0:T(2,128)(2,1)} %reshape.228), calls=%async_computation | async-start | bytes 557056 | tf_op jit(solution)/shard_map/all_to_all | solution.py:10
  77.8 12.1 %copy-start.2 = (bf16[8,64,64]{2,1,0:T(8,128)(2,1)S(1)}, bf16[8,64,64]{2,1,0:T(8,128)(2,1)}, u32[]{:S(2)}) copy-start(bf16[8,64,64]{2,1,0:T(8,128)(2,1)} %param.13) | copy-start | bytes 196612
  89.7 1.5 copy-start.3
  93.1 17.5 %all-to-all-start.1 = ((bf16[32,2,2432]{2,1,0:T(2,128)(2,1)}), bf16[32,2,2432]{2,1,0:T(2,128)(2,1)S(1)}, u32[]{:S(2)}, u32[]{:S(2)}) async-start(bf16[32,2,2432]{2,1,0:T(2,128)(2,1)} %reshape.230), calls=%async_computation.1 | async-start | bytes 622592 | tf_op jit(solution)/shard_map/all_to_all | solution.py:10
  116.4 26.2 %all-to-all-start.2 = ((bf16[32,6,1536]{2,1,0:T(8,128)(2,1)}), bf16[32,6,1536]{2,1,0:T(8,128)(2,1)S(1)}, u32[]{:S(2)}, u32[]{:S(2)}) async-start(bf16[32,6,1536]{2,1,0:T(8,128)(2,1)} %convert_element_type.128), calls=%async_computation.2 | async-start | bytes 1572864 | tf_op jit(solution)/shard_map/all_to_all | solution.py:10
  123.0 64.3 %reduce-scatter.2.cloned.1.call-start = ((), (), s32[]{:S(2)}) async-start(), calls=%async_computation.6 | async-start | bytes 1253376 | tf_op jit(solution)/shard_map/reduce_scatter | solution.py:186
  144.1 47.6 %all-to-all-start.3 = ((f32[32,6,1536]{2,1,0:T(8,128)}), f32[32,6,1536]{2,1,0:T(8,128)S(1)}, u32[]{:S(2)}, u32[]{:S(2)}) async-start(f32[32,6,1536]{2,1,0:T(8,128)} %broadcast_in_dim.9), calls=%async_computation.3 | async-start | bytes 3145728 | tf_op jit(solution)/shard_map/all_to_all | solution.py:10
Sparse Core Ops, SparseCore 0:
  10.7 47.3 all-gather.1
  126.6 60.6 reduce-scatter.1
where the time goes:
time: 201 us; the launch traced here: 200 us
  waiting for transfers between devices  120 us (60%)
  starting transfers between devices  30.3 us (15%)
  local copies, waits for them, and re-layouts  15.6 us (8%)
  matrix products  14.6 us (7%)
  between operations  14.6 us (7%)
  other arithmetic  5.08 us (3%)
    all_gather x1, waiting for transfers between devices, body(): gathered_all = lax.all_gather(packed, 'chan', axis=0, tiled=True)  46.3 us
    all_to_all x4, waiting for transfers between devices, seq_exchange(): return lax.all_to_all(x, 'seq', 0, 0, tiled=True)  39.4 us
    reduce_scatter x1, waiting for transfers between devices, body(): lax.psum_scatter(fac_send.reshape(-1, 128), 'chan', scatter_dimension=0,...  34.6 us
    all_to_all x4, starting transfers between devices, seq_exchange(): return lax.all_to_all(x, 'seq', 0, 0, tiled=True)  30.2 us
  transfers between devices with their start and end apart: 6, of which 5 were waited for; matrix products, arithmetic and copies ran while one was open for 6% of the time, Pallas kernels for 0%

commit v1 on v0

--- a/solution.py
+++ b/solution.py
@@ -4,6 +4,22 @@
 from jax.sharding import PartitionSpec as P
 
 HIGHEST = lax.Precision.HIGHEST
+
+
+def advance_outputs(raw):
+    cores_n = lax.psum(1, axis_name="chan")
+    entries = [(b, (b + 1) % cores_n) for b in range(cores_n)]
+    all_rows = [(b, (b - 1) % cores_n) for b in range(cores_n)]
+    taken_in, y = ([raw], [raw])
+    for _ in range(cores_n // 2):
+        right_arr = lax.ppermute(taken_in[-1], axis_name="chan", perm=entries)
+        taken_in.append(right_arr)
+    for _ in [*range((cores_n - 1) // 2)]:
+        everything = lax.ppermute(y[-1], axis_name="chan", perm=all_rows)
+        y.append(everything)
+    current_block = jnp.concatenate([*taken_in[::-1], *y[1:]], axis=0)
+    n_now = jnp.roll(current_block, (lax.axis_index("chan") - cores_n // 2) * raw.shape[0], 0)
+    return n_now
 
 
 def seq_exchange(x):
@@ -46,7 +62,7 @@
     docs_here = n_doc // n_seq
     me = lax.axis_index("seq")
     packed = jnp.concatenate([tokens, down_latent], axis=1)
-    gathered_all = lax.all_gather(packed, "chan", axis=0, tiled=True)
+    gathered_all = advance_outputs(packed)
     gathered = gathered_all[:, :tok_cols]
     down_full = gathered_all[:, tok_cols:]
     doc_ends = jnp.cumsum(doc_lengths)

time: 201 us -> 203 us (level)
  waiting for transfers between devices: 120 us -> 97.6 us
  starting transfers between devices: 30.3 us -> 51.2 us
  local copies, waits for them, and re-layouts: 15.6 us -> 21.5 us
    all_gather x1 -> x0, waiting for transfers between devices: 46.3 us -> none  [body(): gathered_all = lax.all_gather(packed, 'chan', axis=0, tiled=True)]
    ppermute x0 -> x15, waiting for transfers between devices: none -> 25.9 us  [the longest x8 25.7 us: advance_outputs(): right_arr = lax.ppermute(taken_in[-1], axis_name='chan', perm=entries)]
    ppermute x0 -> x15, starting transfers between devices: none -> 20.8 us  [the longest x7 20.8 us: advance_outputs(): everything = lax.ppermute(y[-1], axis_name='chan', perm=all_rows)]
    all_to_all x4, waiting for transfers between devices: 39.4 us -> 31.8 us  [seq_exchange(): return lax.all_to_all(x, 'seq', 0, 0, tiled=True)]
    reduce_scatter x1, waiting for transfers between devices: 34.6 us -> 39.8 us  [body(): lax.psum_scatter(fac_send.reshape(-1, 128), 'chan', scatter_dimension=0,...]
    unnamed x21 -> x63, local copies, waits for them, and re-layouts: 2.51 us -> 7.58 us
  transfers between devices with their start and end apart: 6 -> 20, of which waited for: 5 -> 13; matrix products, arithmetic and copies ran while one was open for 6% -> 7% of each run, Pallas kernels for 0% -> 0%
where the time goes in v1:
time: 203 us; the launch traced here: 202 us
  waiting for transfers between devices  97.6 us (48%)
  starting transfers between devices  51.2 us (25%)
  local copies, waits for them, and re-layouts  21.5 us (11%)
  between operations  14.8 us (7%)
  matrix products  13.8 us (7%)
  other arithmetic  3.43 us (2%)
    reduce_scatter x1, waiting for transfers between devices, body(): lax.psum_scatter(fac_send.reshape(-1, 128), 'chan', scatter_dimension=0,...  39.8 us
    all_to_all x4, waiting for transfers between devices, seq_exchange(): return lax.all_to_all(x, 'seq', 0, 0, tiled=True)  31.8 us
    all_to_all x4, starting transfers between devices, seq_exchange(): return lax.all_to_all(x, 'seq', 0, 0, tiled=True)  30.3 us
    ppermute x8, waiting for transfers between devices, advance_outputs(): right_arr = lax.ppermute(taken_in[-1], axis_name='chan', perm=entries)  25.7 us
    ppermute x7, starting transfers between devices, advance_outputs(): everything = lax.ppermute(y[-1], axis_name='chan', perm=all_rows)  20.8 us
    unnamed x63, local copies, waits for them, and re-layouts  7.58 us
  transfers between devices with their start and end apart: 20, of which 13 were waited for; matrix products, arithmetic and copies ran while one was open for 7% of the time, Pallas kernels for 0%

profile of v1, /device:TPU:6, one launch (start us, length us, event | category | flops | bytes accessed | tf_op | source)
XLA Modules:
  0.0 202.3 jit_solution(3197806652210643433)
XLA Ops:
  8.9 11.0 %collective-permute-done = bf16[96,640]{1,0:T(8,128)(2,1)S(1)} collective-permute-done((bf16[96,640]{1,0:T(8,128)(2,1)S(1)}, bf16[96,640]{1,0:T(8,128)(2,1)S(1)}, u32[]{:S(2)}, u32[]{:S(2)}) %collective-permute-start) | collective-permute-done | bytes 122912 | tf_op jit(solution)/shard_map/ppermute | solution.py:15
  20.0 3.0 %collective-permute-start.8 = (bf16[96,640]{1,0:T(8,128)(2,1)S(1)}, bf16[96,640]{1,0:T(8,128)(2,1)S(1)}, u32[]{:S(2)}, u32[]{:S(2)}) collective-permute-start(bf16[96,640]{1,0:T(8,128)(2,1)S(1)} %constant_dynamic-update-slice_fusion), channel_id=1, source_target_pairs={{0,15},{1,0},{2,1},{3,2},{4,3},{5,4},{6,5},{7,6},{8,7},{9,8},{10,9... | collective-permute-start | bytes 368648 | tf_op jit(solution)/shard_map/ppermute | solution.py:18
  22.9 2.6 %collective-permute-done.1 = bf16[96,640]{1,0:T(8,128)(2,1)S(1)} collective-permute-done((bf16[96,640]{1,0:T(8,128)(2,1)S(1)}, bf16[96,640]{1,0:T(8,128)(2,1)S(1)}, u32[]{:S(2)}, u32[]{:S(2)}) %collective-permute-start.1) | collective-permute-done | bytes 122912 | tf_op jit(solution)/shard_map/ppermute | solution.py:15
  25.5 3.0 %collective-permute-start.9 = (bf16[96,640]{1,0:T(8,128)(2,1)S(1)}, bf16[96,640]{1,0:T(8,128)(2,1)S(1)}, u32[]{:S(2)}, u32[]{:S(2)}) collective-permute-start(bf16[96,640]{1,0:T(8,128)(2,1)S(1)} %collective-permute-done.8), channel_id=1, source_target_pairs={{0,15},{1,0},{2,1},{3,2},{4,3},{5,4},{6,5},{7,6},{8,7},{9,8},{10,9... | collective-permute-start | bytes 368648 | tf_op jit(solution)/shard_map/ppermute | solution.py:18
  28.4 2.6 %collective-permute-done.2 = bf16[96,640]{1,0:T(8,128)(2,1)S(1)} collective-permute-done((bf16[96,640]{1,0:T(8,128)(2,1)S(1)}, bf16[96,640]{1,0:T(8,128)(2,1)S(1)}, u32[]{:S(2)}, u32[]{:S(2)}) %collective-permute-start.2) | collective-permute-done | bytes 122912 | tf_op jit(solution)/shard_map/ppermute | solution.py:15
  31.0 3.0 %collective-permute-start.10 = (bf16[96,640]{1,0:T(8,128)(2,1)S(1)}, bf16[96,640]{1,0:T(8,128)(2,1)S(1)}, u32[]{:S(2)}, u32[]{:S(2)}) collective-permute-start(bf16[96,640]{1,0:T(8,128)(2,1)S(1)} %collective-permute-done.9), channel_id=1, source_target_pairs={{0,15},{1,0},{2,1},{3,2},{4,3},{5,4},{6,5},{7,6},{8,7},{9,8},{10,9... | collective-permute-start | bytes 368648 | tf_op jit(solution)/shard_map/ppermute | solution.py:18
  33.9 2.6 %collective-permute-done.3 = bf16[96,640]{1,0:T(8,128)(2,1)S(1)} collective-permute-done((bf16[96,640]{1,0:T(8,128)(2,1)S(1)}, bf16[96,640]{1,0:T(8,128)(2,1)S(1)}, u32[]{:S(2)}, u32[]{:S(2)}) %collective-permute-start.3) | collective-permute-done | bytes 122912 | tf_op jit(solution)/shard_map/ppermute | solution.py:15
  36.5 3.0 %collective-permute-start.11 = (bf16[96,640]{1,0:T(8,128)(2,1)S(1)}, bf16[96,640]{1,0:T(8,128)(2,1)S(1)}, u32[]{:S(2)}, u32[]{:S(2)}) collective-permute-start(bf16[96,640]{1,0:T(8,128)(2,1)S(1)} %collective-permute-done.10), channel_id=1, source_target_pairs={{0,15},{1,0},{2,1},{3,2},{4,3},{5,4},{6,5},{7,6},{8,7},{9,8},{10,9... | collective-permute-start | bytes 368648 | tf_op jit(solution)/shard_map/ppermute | solution.py:18
  39.5 2.6 %collective-permute-done.4 = bf16[96,640]{1,0:T(8,128)(2,1)S(1)} collective-permute-done((bf16[96,640]{1,0:T(8,128)(2,1)S(1)}, bf16[96,640]{1,0:T(8,128)(2,1)S(1)}, u32[]{:S(2)}, u32[]{:S(2)}) %collective-permute-start.4) | collective-permute-done | bytes 122912 | tf_op jit(solution)/shard_map/ppermute | solution.py:15
  42.0 3.0 %collective-permute-start.12 = (bf16[96,640]{1,0:T(8,128)(2,1)S(1)}, bf16[96,640]{1,0:T(8,128)(2,1)S(1)}, u32[]{:S(2)}, u32[]{:S(2)}) collective-permute-start(bf16[96,640]{1,0:T(8,128)(2,1)S(1)} %collective-permute-done.11), channel_id=1, source_target_pairs={{0,15},{1,0},{2,1},{3,2},{4,3},{5,4},{6,5},{7,6},{8,7},{9,8},{10,9... | collective-permute-start | bytes 368648 | tf_op jit(solution)/shard_map/ppermute | solution.py:18
  45.0 2.6 %collective-permute-done.5 = bf16[96,640]{1,0:T(8,128)(2,1)S(1)} collective-permute-done((bf16[96,640]{1,0:T(8,128)(2,1)S(1)}, bf16[96,640]{1,0:T(8,128)(2,1)S(1)}, u32[]{:S(2)}, u32[]{:S(2)}) %collective-permute-start.5) | collective-permute-done | bytes 122912 | tf_op jit(solution)/shard_map/ppermute | solution.py:15
  49.2 3.0 %collective-permute-start.13 = (bf16[96,640]{1,0:T(8,128)(2,1)S(1)}, bf16[96,640]{1,0:T(8,128)(2,1)S(1)}, u32[]{:S(2)}, u32[]{:S(2)}) collective-permute-start(bf16[96,640]{1,0:T(8,128)(2,1)S(1)} %collective-permute-done.12), channel_id=1, source_target_pairs={{0,15},{1,0},{2,1},{3,2},{4,3},{5,4},{6,5},{7,6},{8,7},{9,8},{10,9... | collective-permute-start | bytes 368648 | tf_op jit(solution)/shard_map/ppermute | solution.py:18
  54.6 3.1 %collective-permute-start.14 = (bf16[96,640]{1,0:T(8,128)(2,1)S(1)}, bf16[96,640]{1,0:T(8,128)(2,1)S(1)}, u32[]{:S(2)}, u32[]{:S(2)}) collective-permute-start(bf16[96,640]{1,0:T(8,128)(2,1)S(1)} %collective-permute-done.13), channel_id=1, source_target_pairs={{0,15},{1,0},{2,1},{3,2},{4,3},{5,4},{6,5},{7,6},{8,7},{9,8},{10,9... | collective-permute-start | bytes 368648 | tf_op jit(solution)/shard_map/ppermute | solution.py:18
  63.7 2.0 convolution_convert_fusion.3
  66.9 2.4 %fusion.3 = f32[128,512]{1,0:T(8,128)S(1)} fusion(bf16[3072,640]{1,0:T(8,128)(2,1)} %copy-done.1, s32[]{:T(128)S(6)} %select_n.17, s32[]{:T(128)S(6)} %add.52), kind=kOutput, calls=%fused_computation.14 | convolution fusion | flops 201326592 | bytes 2229760 | tf_op jit(solution)/shard_map/ct,cl->lt/dot_general | solution.py:79
  71.8 10.2 %all-to-all-start = ((bf16[32,2,2176]{2,1,0:T(2,128)(2,1)}), bf16[32,2,2176]{2,1,0:T(2,128)(2,1)S(1)}, u32[]{:S(2)}, u32[]{:S(2)}) async-start(bf16[32,2,2176]{2,1,0:T(2,128)(2,1)} %reshape.228), calls=%async_computation | async-start | bytes 557056 | tf_op jit(solution)/shard_map/all_to_all | solution.py:26
  82.2 9.2 %all-to-all-done = bf16[32,2,2176]{2,1,0:T(2,128)(2,1)S(1)} async-done(((bf16[32,2,2176]{2,1,0:T(2,128)(2,1)}), bf16[32,2,2176]{2,1,0:T(2,128)(2,1)S(1)}, u32[]{:S(2)}, u32[]{:S(2)}) %all-to-all-start) | async-done | bytes 278560 | tf_op jit(solution)/shard_map/all_to_all | solution.py:26
  95.6 6.4 %all-to-all-start.1 = ((bf16[32,2,2432]{2,1,0:T(2,128)(2,1)}), bf16[32,2,2432]{2,1,0:T(2,128)(2,1)S(1)}, u32[]{:S(2)}, u32[]{:S(2)}) async-start(bf16[32,2,2432]{2,1,0:T(2,128)(2,1)} %reshape.230), calls=%async_computation.1 | async-start | bytes 622592 | tf_op jit(solution)/shard_map/all_to_all | solution.py:26
  102.5 9.2 %all-to-all-done.1 = bf16[32,2,2432]{2,1,0:T(2,128)(2,1)S(1)} async-done(((bf16[32,2,2432]{2,1,0:T(2,128)(2,1)}), bf16[32,2,2432]{2,1,0:T(2,128)(2,1)S(1)}, u32[]{:S(2)}, u32[]{:S(2)}) %all-to-all-start.1) | async-done | bytes 311328 | tf_op jit(solution)/shard_map/all_to_all | solution.py:26
  114.7 2.1 %convolution_convert_fusion = bf16[192,1536]{1,0:T(8,128)(2,1)S(1)} fusion(bf16[3072,640]{1,0:T(8,128)(2,1)} %copy-done.1, s32[]{:T(128)S(6)} %select_n.17, bf16[96,512]{1,0:T(8,128)(2,1)S(1)} %bitcast.132, bf16[96,512]{1,0:T(8,128)(2,1)S(1)} %get-tuple-element.9), kind=kOutput, calls=%fused_computation | convolution fusion | flops 302678016 | bytes 2359300 | tf_op jit(solution)/shard_map/ot,it->oi/dot_general | solution.py:183
  117.9 6.2 %all-to-all-start.2 = ((bf16[32,6,1536]{2,1,0:T(8,128)(2,1)}), bf16[32,6,1536]{2,1,0:T(8,128)(2,1)S(1)}, u32[]{:S(2)}, u32[]{:S(2)}) async-start(bf16[32,6,1536]{2,1,0:T(8,128)(2,1)} %convert_element_type.128), calls=%async_computation.2 | async-start | bytes 1572864 | tf_op jit(solution)/shard_map/all_to_all | solution.py:26
  125.6 13.4 %all-to-all-done.2 = bf16[32,6,1536]{2,1,0:T(8,128)(2,1)S(1)} async-done(((bf16[32,6,1536]{2,1,0:T(8,128)(2,1)}), bf16[32,6,1536]{2,1,0:T(8,128)(2,1)S(1)}, u32[]{:S(2)}, u32[]{:S(2)}) %all-to-all-start.2) | async-done | bytes 589856 | tf_op jit(solution)/shard_map/all_to_all | solution.py:26
  140.5 7.4 %all-to-all-start.3 = ((f32[32,6,1536]{2,1,0:T(8,128)}), f32[32,6,1536]{2,1,0:T(8,128)S(1)}, u32[]{:S(2)}, u32[]{:S(2)}) async-start(f32[32,6,1536]{2,1,0:T(8,128)} %broadcast_in_dim.9), calls=%async_computation.3 | async-start | bytes 3145728 | tf_op jit(solution)/shard_map/all_to_all | solution.py:26
  149.3 39.8 %reduce-scatter.2.cloned.1.call-done = f32[144,128]{1,0:T(8,128)} async-done(((f32[2304,128]{1,0:T(8,128)}), f32[144,128]{1,0:T(8,128)}) %reduce-scatter.2.cloned.1.call-update) | async-done | bytes 73744 | tf_op jit(solution)/shard_map/reduce_scatter | solution.py:202
  (168 shorter events, 34.5 us)
Async XLA Ops:
  7.2 55.7 %copy-start = (bf16[96,1536]{1,0:T(8,128)(2,1)S(1)}, bf16[96,1536]{1,0:T(8,128)(2,1)}, u32[]{:S(2)}) copy-start(bf16[96,1536]{1,0:T(8,128)(2,1)} %param.10) | copy-start | bytes 884740
  7.2 53.6 %copy-start.3 = (bf16[96,512]{1,0:T(8,128)(2,1)S(1)}, bf16[96,512]{1,0:T(8,128)(2,1)}, u32[]{:S(2)}) copy-start(bf16[96,512]{1,0:T(8,128)(2,1)} %param.9) | copy-start | bytes 294916
  7.2 53.6 %copy-start.6 = (bf16[96,128]{1,0:T(8,128)(2,1)S(1)}, bf16[96,128]{1,0:T(8,128)(2,1)}, u32[]{:S(2)}) copy-start(bf16[96,128]{1,0:T(8,128)(2,1)} %param.14) | copy-start | bytes 73732
  8.9 11.0 %collective-permute-start = (bf16[96,640]{1,0:T(8,128)(2,1)S(1)}, bf16[96,640]{1,0:T(8,128)(2,1)S(1)}, u32[]{:S(2)}, u32[]{:S(2)}) collective-permute-start(bf16[96,640]{1,0:T(8,128)(2,1)S(1)} %constant_dynamic-update-slice_fusion), channel_id=1, source_target_pairs={{0,1},{1,2},{2,3},{3,4},{4,5},{5,6},{6,7},{7,8},{8,9},{9,10},{10,1... | collective-permute-start | bytes 368648 | tf_op jit(solution)/shard_map/ppermute | solution.py:15
  19.9 5.5 %collective-permute-start.1 = (bf16[96,640]{1,0:T(8,128)(2,1)S(1)}, bf16[96,640]{1,0:T(8,128)(2,1)S(1)}, u32[]{:S(2)}, u32[]{:S(2)}) collective-permute-start(bf16[96,640]{1,0:T(8,128)(2,1)S(1)} %collective-permute-done), channel_id=1, source_target_pairs={{0,1},{1,2},{2,3},{3,4},{4,5},{5,6},{6,7},{7,8},{8,9},{9,10},{10,1... | collective-permute-start | bytes 368648 | tf_op jit(solution)/shard_map/ppermute | solution.py:15
  20.0 5.5 %collective-permute-start.8 = (bf16[96,640]{1,0:T(8,128)(2,1)S(1)}, bf16[96,640]{1,0:T(8,128)(2,1)S(1)}, u32[]{:S(2)}, u32[]{:S(2)}) collective-permute-start(bf16[96,640]{1,0:T(8,128)(2,1)S(1)} %constant_dynamic-update-slice_fusion), channel_id=1, source_target_pairs={{0,15},{1,0},{2,1},{3,2},{4,3},{5,4},{6,5},{7,6},{8,7},{9,8},{10,9... | collective-permute-start | bytes 368648 | tf_op jit(solution)/shard_map/ppermute | solution.py:18
  25.5 5.5 %collective-permute-start.2 = (bf16[96,640]{1,0:T(8,128)(2,1)S(1)}, bf16[96,640]{1,0:T(8,128)(2,1)S(1)}, u32[]{:S(2)}, u32[]{:S(2)}) collective-permute-start(bf16[96,640]{1,0:T(8,128)(2,1)S(1)} %collective-permute-done.1), channel_id=1, source_target_pairs={{0,1},{1,2},{2,3},{3,4},{4,5},{5,6},{6,7},{7,8},{8,9},{9,10},{10,1... | collective-permute-start | bytes 368648 | tf_op jit(solution)/shard_map/ppermute | solution.py:15
  25.5 5.5 %collective-permute-start.9 = (bf16[96,640]{1,0:T(8,128)(2,1)S(1)}, bf16[96,640]{1,0:T(8,128)(2,1)S(1)}, u32[]{:S(2)}, u32[]{:S(2)}) collective-permute-start(bf16[96,640]{1,0:T(8,128)(2,1)S(1)} %collective-permute-done.8), channel_id=1, source_target_pairs={{0,15},{1,0},{2,1},{3,2},{4,3},{5,4},{6,5},{7,6},{8,7},{9,8},{10,9... | collective-permute-start | bytes 368648 | tf_op jit(solution)/shard_map/ppermute | solution.py:18
  31.0 5.5 %collective-permute-start.3 = (bf16[96,640]{1,0:T(8,128)(2,1)S(1)}, bf16[96,640]{1,0:T(8,128)(2,1)S(1)}, u32[]{:S(2)}, u32[]{:S(2)}) collective-permute-start(bf16[96,640]{1,0:T(8,128)(2,1)S(1)} %collective-permute-done.2), channel_id=1, source_target_pairs={{0,1},{1,2},{2,3},{3,4},{4,5},{5,6},{6,7},{7,8},{8,9},{9,10},{10,1... | collective-permute-start | bytes 368648 | tf_op jit(solution)/shard_map/ppermute | solution.py:15
  31.0 5.5 %collective-permute-start.10 = (bf16[96,640]{1,0:T(8,128)(2,1)S(1)}, bf16[96,640]{1,0:T(8,128)(2,1)S(1)}, u32[]{:S(2)}, u32[]{:S(2)}) collective-permute-start(bf16[96,640]{1,0:T(8,128)(2,1)S(1)} %collective-permute-done.9), channel_id=1, source_target_pairs={{0,15},{1,0},{2,1},{3,2},{4,3},{5,4},{6,5},{7,6},{8,7},{9,8},{10,9... | collective-permute-start | bytes 368648 | tf_op jit(solution)/shard_map/ppermute | solution.py:18
  36.5 5.5 %collective-permute-start.4 = (bf16[96,640]{1,0:T(8,128)(2,1)S(1)}, bf16[96,640]{1,0:T(8,128)(2,1)S(1)}, u32[]{:S(2)}, u32[]{:S(2)}) collective-permute-start(bf16[96,640]{1,0:T(8,128)(2,1)S(1)} %collective-permute-done.3), channel_id=1, source_target_pairs={{0,1},{1,2},{2,3},{3,4},{4,5},{5,6},{6,7},{7,8},{8,9},{9,10},{10,1... | collective-permute-start | bytes 368648 | tf_op jit(solution)/shard_map/ppermute | solution.py:15
  36.5 5.5 %collective-permute-start.11 = (bf16[96,640]{1,0:T(8,128)(2,1)S(1)}, bf16[96,640]{1,0:T(8,128)(2,1)S(1)}, u32[]{:S(2)}, u32[]{:S(2)}) collective-permute-start(bf16[96,640]{1,0:T(8,128)(2,1)S(1)} %collective-permute-done.10), channel_id=1, source_target_pairs={{0,15},{1,0},{2,1},{3,2},{4,3},{5,4},{6,5},{7,6},{8,7},{9,8},{10,9... | collective-permute-start | bytes 368648 | tf_op jit(solution)/shard_map/ppermute | solution.py:18
  42.0 5.5 %collective-permute-start.5 = (bf16[96,640]{1,0:T(8,128)(2,1)S(1)}, bf16[96,640]{1,0:T(8,128)(2,1)S(1)}, u32[]{:S(2)}, u32[]{:S(2)}) collective-permute-start(bf16[96,640]{1,0:T(8,128)(2,1)S(1)} %collective-permute-done.4), channel_id=1, source_target_pairs={{0,1},{1,2},{2,3},{3,4},{4,5},{5,6},{6,7},{7,8},{8,9},{9,10},{10,1... | collective-permute-start | bytes 368648 | tf_op jit(solution)/shard_map/ppermute | solution.py:15
  42.0 7.1 %collective-permute-start.12 = (bf16[96,640]{1,0:T(8,128)(2,1)S(1)}, bf16[96,640]{1,0:T(8,128)(2,1)S(1)}, u32[]{:S(2)}, u32[]{:S(2)}) collective-permute-start(bf16[96,640]{1,0:T(8,128)(2,1)S(1)} %collective-permute-done.11), channel_id=1, source_target_pairs={{0,15},{1,0},{2,1},{3,2},{4,3},{5,4},{6,5},{7,6},{8,7},{9,8},{10,9... | collective-permute-start | bytes 368648 | tf_op jit(solution)/shard_map/ppermute | solution.py:18
  47.5 5.5 %collective-permute-start.6 = (bf16[96,640]{1,0:T(8,128)(2,1)S(1)}, bf16[96,640]{1,0:T(8,128)(2,1)S(1)}, u32[]{:S(2)}, u32[]{:S(2)}) collective-permute-start(bf16[96,640]{1,0:T(8,128)(2,1)S(1)} %collective-permute-done.5), channel_id=1, source_target_pairs={{0,1},{1,2},{2,3},{3,4},{4,5},{5,6},{6,7},{7,8},{8,9},{9,10},{10,1... | collective-permute-start | bytes 368648 | tf_op jit(solution)/shard_map/ppermute | solution.py:15
  49.2 5.4 %collective-permute-start.13 = (bf16[96,640]{1,0:T(8,128)(2,1)S(1)}, bf16[96,640]{1,0:T(8,128)(2,1)S(1)}, u32[]{:S(2)}, u32[]{:S(2)}) collective-permute-start(bf16[96,640]{1,0:T(8,128)(2,1)S(1)} %collective-permute-done.12), channel_id=1, source_target_pairs={{0,15},{1,0},{2,1},{3,2},{4,3},{5,4},{6,5},{7,6},{8,7},{9,8},{10,9... | collective-permute-start | bytes 368648 | tf_op jit(solution)/shard_map/ppermute | solution.py:18
  53.0 5.5 %collective-permute-start.7 = (bf16[96,640]{1,0:T(8,128)(2,1)S(1)}, bf16[96,640]{1,0:T(8,128)(2,1)S(1)}, u32[]{:S(2)}, u32[]{:S(2)}) collective-permute-start(bf16[96,640]{1,0:T(8,128)(2,1)S(1)} %collective-permute-done.6), channel_id=1, source_target_pairs={{0,1},{1,2},{2,3},{3,4},{4,5},{5,6},{6,7},{7,8},{8,9},{9,10},{10,1... | collective-permute-start | bytes 368648 | tf_op jit(solution)/shard_map/ppermute | solution.py:15
  54.6 6.0 %collective-permute-start.14 = (bf16[96,640]{1,0:T(8,128)(2,1)S(1)}, bf16[96,640]{1,0:T(8,128)(2,1)S(1)}, u32[]{:S(2)}, u32[]{:S(2)}) collective-permute-start(bf16[96,640]{1,0:T(8,128)(2,1)S(1)} %collective-permute-done.13), channel_id=1, source_target_pairs={{0,15},{1,0},{2,1},{3,2},{4,3},{5,4},{6,5},{7,6},{8,7},{9,8},{10,9... | collective-permute-start | bytes 368648 | tf_op jit(solution)/shard_map/ppermute | solution.py:18
  66.9 25.5 %copy-start.4 = (bf16[8,64,64]{2,1,0:T(8,128)(2,1)S(1)}, bf16[8,64,64]{2,1,0:T(8,128)(2,1)}, u32[]{:S(2)}) copy-start(bf16[8,64,64]{2,1,0:T(8,128)(2,1)} %param.13) | copy-start | bytes 196612
  71.8 19.5 %all-to-all-start = ((bf16[32,2,2176]{2,1,0:T(2,128)(2,1)}), bf16[32,2,2176]{2,1,0:T(2,128)(2,1)S(1)}, u32[]{:S(2)}, u32[]{:S(2)}) async-start(bf16[32,2,2176]{2,1,0:T(2,128)(2,1)} %reshape.228), calls=%async_computation | async-start | bytes 557056 | tf_op jit(solution)/shard_map/all_to_all | solution.py:26
  95.6 16.1 %all-to-all-start.1 = ((bf16[32,2,2432]{2,1,0:T(2,128)(2,1)}), bf16[32,2,2432]{2,1,0:T(2,128)(2,1)S(1)}, u32[]{:S(2)}, u32[]{:S(2)}) async-start(bf16[32,2,2432]{2,1,0:T(2,128)(2,1)} %reshape.230), calls=%async_computation.1 | async-start | bytes 622592 | tf_op jit(solution)/shard_map/all_to_all | solution.py:26
  117.9 21.1 %all-to-all-start.2 = ((bf16[32,6,1536]{2,1,0:T(8,128)(2,1)}), bf16[32,6,1536]{2,1,0:T(8,128)(2,1)S(1)}, u32[]{:S(2)}, u32[]{:S(2)}) async-start(bf16[32,6,1536]{2,1,0:T(8,128)(2,1)} %convert_element_type.128), calls=%async_computation.2 | async-start | bytes 1572864 | tf_op jit(solution)/shard_map/all_to_all | solution.py:26
  124.2 64.9 %reduce-scatter.2.cloned.1.call-start = ((), (), s32[]{:S(2)}) async-start(), calls=%async_computation.5 | async-start | bytes 1253376 | tf_op jit(solution)/shard_map/reduce_scatter | solution.py:202
  140.5 53.0 %all-to-all-start.3 = ((f32[32,6,1536]{2,1,0:T(8,128)}), f32[32,6,1536]{2,1,0:T(8,128)S(1)}, u32[]{:S(2)}, u32[]{:S(2)}) async-start(f32[32,6,1536]{2,1,0:T(8,128)} %broadcast_in_dim.9), calls=%async_computation.3 | async-start | bytes 3145728 | tf_op jit(solution)/shard_map/all_to_all | solution.py:26
  (6 other events, 58.7 us)
Sparse Core Ops, SparseCore 0:
  127.8 61.2 reduce-scatter.1
